TPU v7x, 128 devices: a whole 4x4x4 slice. The times are simulated.
128 devices in a mesh: row: 16 (over z, x), col: 8 (over y, core).
Axes of the slice: x: 4, y: 4, z: 4, core: 2. Of those that a mesh axis runs over, the one named last changes fastest.
Arguments:
- residual: bfloat16 [512, 1024, 256], P(('row', 'col')), may hold values from -6 to 6
- interface_inverse: bfloat16 [512, 1024, 1024], P(('row', 'col'))
- modes: bfloat16 [512, 1024, 32], P(('row', 'col')), may hold values from -0.375 to 0.375
- coarse_map: int32 [16384], P(('row', 'col')), may hold values from 0 to 16383, each once
- coarse_inverse: bfloat16 [16384, 16384], P('row', 'col')
- neighbours: int32 [512, 2], P(('row', 'col')), may hold values from 0 to 511, as said below
- block_sizes: int32 [512, 2], P(('row', 'col')), may hold values from 128 to 256, as said below
- block_offsets: int32 [512, 2], P(('row', 'col')), may hold values from 0 to 384, as said below
Outputs:
- preconditioned: bfloat16 [512, 1024, 256], P(('row', 'col'))
Inputs may be any that keep to these rules, and one draw needn't show every extreme that they name: In round k the neighbour of subdomain s is (g XOR a_k) * 4 + (s mod 4) XOR b_k with g = s div 4, where a_k, b_k are the same for all subdomains, a_k is nonzero and a_0 differs from a_1; neighbours are mutual. `block_sizes`: each is 128 or 256, and equal for both sides of a shared block. `block_offsets`: the block of round k lies inside rows [k * 256, (k + 1) * 256) and starts at k * 256 or k * 256 + 256 // 2.
All inputs are finite; a program needn't handle non-finite values.
Results may differ from a plain program's by a relative error of at most 0.0052.
Values may be sent and summed in bfloat16 or wider, within the bound.
No kernel may reach another device: no remote copies, remote signals or barrier semaphores. Data moves between devices by JAX's collectives and lax.ppermute only.
A program may use at most 128 MiB of HBM per device.

v0:
```python
import jax
import jax.numpy as jnp
from jax import lax
from jax.sharding import PartitionSpec as P

MODES = 32
SHARE = 256


def from_partner(value, axis, apart):
    return lax.ppermute(value, axis, [(i, i ^ 1 << apart) for i in range(lax.axis_size(axis))])


def travel(carried, partner_bits):
    total_bits = lax.axis_size(("row", "col")).bit_length() - 1
    for level in range(total_bits):
        other = from_partner(carried, ("row", "col"), level)
        chosen = jnp.bitwise_and(jnp.right_shift(partner_bits, level), 1) == 1
        carried = jnp.where(chosen, other, carried)
    return carried


def neighbour_sum(field, neighbours, block_sizes, block_offsets):
    count = field.shape[0]
    cases = field.shape[2]
    trace_len = field.shape[1]
    half_share = SHARE // 2
    device_index = lax.axis_index(("row", "col"))
    row_index = jnp.arange(SHARE)
    summed = field.astype(jnp.float32)
    for which in range(2):
        start = which * SHARE
        region = field[:, start : start + SHARE]
        relative = block_offsets[:, which] - start
        shifted = jnp.concatenate(
            [region[:, half_share:], jnp.zeros((count, half_share, cases), jnp.bfloat16)], 1
        )
        aligned = jnp.where((relative == 0)[:, None, None], region, shifted)
        inside = (row_index[None, :] < block_sizes[:, which][:, None])[:, :, None]
        aligned = jnp.where(inside, aligned, jnp.zeros_like(aligned))
        partner_bits = jnp.bitwise_xor(neighbours[0, which] // count, device_index)
        received = travel(aligned, partner_bits)
        arrived = jnp.take(received, neighbours[:, which] % count, axis=0)
        moved = jnp.concatenate(
            [jnp.zeros((count, half_share, cases), jnp.bfloat16), arrived[:, : SHARE - half_share]],
            1,
        )
        placed = jnp.where((relative == 0)[:, None, None], arrived, moved)
        summed = summed + jnp.pad(
            placed.astype(jnp.float32), ((0, 0), (start, trace_len - start - SHARE), (0, 0))
        )
    return summed


def weights_of(block_sizes, block_offsets, trace_len):
    trace_rows = jnp.arange(trace_len)
    covered = jnp.zeros((block_sizes.shape[0], trace_len), jnp.float32)
    for which in range(2):
        lower = block_offsets[:, which][:, None]
        upper = lower + block_sizes[:, which][:, None]
        covered = covered + jnp.where(
            (trace_rows[None, :] >= lower) & (trace_rows[None, :] < upper), 1.0, 0.0
        ).astype(jnp.float32)
    return 1.0 / (1.0 + covered)


def shards(
    residual,
    interface_inverse,
    modes,
    coarse_map,
    coarse_inverse,
    neighbours,
    block_sizes,
    block_offsets,
):
    count = residual.shape[0]
    trace_len = residual.shape[1]
    cases = residual.shape[2]
    omega = weights_of(block_sizes, block_offsets, trace_len)
    weighted = (
        omega[:, :, None] * neighbour_sum(residual, neighbours, block_sizes, block_offsets)
    ).astype(jnp.bfloat16)
    local_part = jnp.einsum(
        "sij,sjr->sir", interface_inverse, weighted, preferred_element_type=jnp.float32
    )
    restricted = jnp.einsum(
        "swm,swr->smr", modes, weighted, preferred_element_type=jnp.float32
    ).astype(jnp.bfloat16)
    restricted = restricted.reshape(count * MODES, cases)
    all_rhs, all_map = (
        lax.all_gather(restricted, ("row", "col"), axis=0, tiled=True),
        lax.all_gather(coarse_map, ("row", "col"), axis=0, tiled=True),
    )
    coarse_rhs = jnp.zeros((all_map.shape[0], cases), jnp.bfloat16).at[all_map].set(all_rhs)
    columns = coarse_inverse.shape[1]
    column_part = lax.dynamic_slice_in_dim(coarse_rhs, lax.axis_index("col") * columns, columns, 0)
    partial_sum = jnp.dot(coarse_inverse, column_part, preferred_element_type=jnp.float32)
    own_rows = lax.psum_scatter(partial_sum, "col", scatter_dimension=0, tiled=True).astype(
        jnp.bfloat16
    )
    coarse_full = lax.all_gather(own_rows, ("row", "col"), axis=0, tiled=True)
    picked = jnp.take(coarse_full, coarse_map, axis=0).reshape(count, MODES, cases)
    prolonged = local_part + jnp.einsum(
        "swm,smr->swr", modes, picked, preferred_element_type=jnp.float32
    )
    corrected = (omega[:, :, None] * prolonged).astype(jnp.bfloat16)
    return neighbour_sum(corrected, neighbours, block_sizes, block_offsets).astype(jnp.bfloat16)


def solution(mesh):
    return jax.shard_map(
        shards,
        mesh=mesh,
        in_specs=(
            P(("row", "col"), None, None),
            P(("row", "col"), None, None),
            P(("row", "col"), None, None),
            P(("row", "col")),
            P("row", "col"),
            P(("row", "col"), None),
            P(("row", "col"), None),
            P(("row", "col"), None),
        ),
        out_specs=P(("row", "col"), None, None),
        check_vma=False,
    )
```

profile of v0, /device:TPU:0, one launch (start us, length us, event | category | flops | bytes accessed | tf_op | source)
XLA Modules:
  0.0 567.4 jit_solution(5247554139306587757)
XLA Ops:
  22.8 9.1 %collective-permute-done.1 = bf16[4,256,256]{1,2,0:T(8,128)(2,1)} collective-permute-done((bf16[4,256,256]{1,2,0:T(8,128)(2,1)S(1)}, bf16[4,256,256]{1,2,0:T(8,128)(2,1)}, u32[]{:S(2)}, u32[]{:S(2)}) %collective-permute-start.1) | collective-permute-done | bytes 524320 | tf_op jit(solution)/shard_map/ppermute | solution.py:11
  47.6 9.2 %collective-permute-done.2 = bf16[4,256,256]{1,2,0:T(8,128)(2,1)S(1)} collective-permute-done((bf16[4,256,256]{1,2,0:T(8,128)(2,1)}, bf16[4,256,256]{1,2,0:T(8,128)(2,1)S(1)}, u32[]{:S(2)}, u32[]{:S(2)}) %collective-permute-start.2) | collective-permute-done | bytes 524320 | tf_op jit(solution)/shard_map/ppermute | solution.py:11
  60.2 7.1 %collective-permute-done.9 = bf16[4,256,256]{1,2,0:T(8,128)(2,1)} collective-permute-done((bf16[4,256,256]{1,2,0:T(8,128)(2,1)S(1)}, bf16[4,256,256]{1,2,0:T(8,128)(2,1)}, u32[]{:S(2)}, u32[]{:S(2)}) %collective-permute-start.9) | collective-permute-done | bytes 524320 | tf_op jit(solution)/shard_map/ppermute | solution.py:11
  77.2 7.0 %collective-permute-done.10 = bf16[4,256,256]{1,2,0:T(8,128)(2,1)} collective-permute-done((bf16[4,256,256]{1,2,0:T(8,128)(2,1)S(1)}, bf16[4,256,256]{1,2,0:T(8,128)(2,1)}, u32[]{:S(2)}, u32[]{:S(2)}) %collective-permute-start.10) | collective-permute-done | bytes 524320 | tf_op jit(solution)/shard_map/ppermute | solution.py:11
  88.5 9.2 %collective-permute-done.4 = bf16[4,256,256]{1,2,0:T(8,128)(2,1)} collective-permute-done((bf16[4,256,256]{1,2,0:T(8,128)(2,1)S(1)}, bf16[4,256,256]{1,2,0:T(8,128)(2,1)}, u32[]{:S(2)}, u32[]{:S(2)}) %collective-permute-start.4) | collective-permute-done | bytes 524320 | tf_op jit(solution)/shard_map/ppermute | solution.py:11
  114.4 7.7 %collective-permute-done.12 = bf16[4,256,256]{1,2,0:T(8,128)(2,1)} collective-permute-done((bf16[4,256,256]{1,2,0:T(8,128)(2,1)S(1)}, bf16[4,256,256]{1,2,0:T(8,128)(2,1)}, u32[]{:S(2)}, u32[]{:S(2)}) %collective-permute-start.12) | collective-permute-done | bytes 524320 | tf_op jit(solution)/shard_map/ppermute | solution.py:11
  127.9 8.9 %collective-permute-done.6 = bf16[4,256,256]{1,2,0:T(8,128)(2,1)} collective-permute-done((bf16[4,256,256]{1,2,0:T(8,128)(2,1)S(1)}, bf16[4,256,256]{1,2,0:T(8,128)(2,1)}, u32[]{:S(2)}, u32[]{:S(2)}) %collective-permute-start.6) | collective-permute-done | bytes 524320 | tf_op jit(solution)/shard_map/ppermute | solution.py:11
  151.1 27.7 %all-gather = s32[128,1,128]{2,1,0:T(1,128)S(1)} all-gather(s32[1,1,128]{2,1,0:T(1,128)S(1)} %bitcast.41), channel_id=1, replica_groups=mesh['row'=16,'col'=8] {'row','col'}, dimensions={0}, use_global_device_ids=true | all-gather | bytes 66048 | tf_op jit(solution)/shard_map/all_gather | solution.py:93
  178.9 36.6 %all-gather.4.cloned.1.call-done = bf16[16384,256]{1,0:T(8,128)(2,1)} async-done(((bf16[128,256]{1,0:T(8,128)(2,1)}), bf16[16384,256]{1,0:T(8,128)(2,1)}) %all-gather.4.cloned.1.call-update) | async-done | bytes 8388624 | tf_op jit(solution)/shard_map/all_gather | solution.py:92
  215.5 74.2 %scatter_custom_fusion = bf16[16384,256]{1,0:T(8,128)(2,1)} fusion(s32[16384]{0:T(1024)S(1)} %compare_select_fusion, bf16[16384,256]{1,0:T(8,128)(2,1)} %all-gather.4.cloned.1.call-done, bf16[]{:T(256)} %constant.108.clone.1), kind=kCustom, calls=%fused_computation.8 | custom fusion | bytes 8389120 | tf_op jit(solution)/shard_map/scatter | solution.py:95
  294.8 29.3 %reduce-scatter.2.cloned.1.call-done = f32[128,256]{0,1:T(8,128)} async-done(((f32[1024,256]{0,1:T(8,128)}), f32[128,256]{0,1:T(8,128)}) %reduce-scatter.2.cloned.1.call-update) | async-done | bytes 131088 | tf_op jit(solution)/shard_map/reduce_scatter | solution.py:99
  325.8 7.7 %fusion.8 = f32[4,256,1024]{2,1,0:T(8,128)} fusion(bf16[4,1024,1024]{2,1,0:T(8,128)(2,1)} %param.11, bf16[4,1024,256]{1,2,0:T(8,128)(2,1)S(1)} %copy.17, bf16[4,256,256]{1,2,0:T(8,128)(2,1)S(1)} %pad_select_fusion.2, bf16[4,256,256]{1,2,0:T(8,128)(2,1)S(1)} %copy-done.4, f32[4,1024]{1,0:T(4,128)S(1)} %add_divide_fusion), kind=kOutput, calls=%fused_computation.59 | convolution fusion | flops 2154823680 | bytes 15745024 | tf_op jit(solution)/shard_map/sij,sjr->sir/dot_general | solution.py:84
  333.5 71.5 %all-gather.6.cloned.1.call-done = bf16[16384,256]{0,1:T(8,128)(2,1)} async-done(((bf16[128,256]{0,1:T(8,128)(2,1)}), bf16[16384,256]{0,1:T(8,128)(2,1)}) %all-gather.6.cloned.1.call-update) | async-done | bytes 8388624 | tf_op jit(solution)/shard_map/all_gather | solution.py:102
  405.0 11.9 %copy.23 = bf16[16384,256]{1,0:T(8,128)(2,1)} copy(bf16[16384,256]{0,1:T(8,128)(2,1)} %all-gather.6.cloned.1.call-done) | data formatting | bytes 16777216 | tf_op jit(solution)/shard_map/all_gather | solution.py:102
  430.2 12.5 %collective-permute-done.15 = bf16[4,256,256]{1,2,0:T(8,128)(2,1)S(1)} collective-permute-done((bf16[4,256,256]{1,2,0:T(8,128)(2,1)S(1)}, bf16[4,256,256]{1,2,0:T(8,128)(2,1)S(1)}, u32[]{:S(2)}, u32[]{:S(2)}) %collective-permute-start.15) | collective-permute-done | bytes 524320 | tf_op jit(solution)/shard_map/ppermute | solution.py:11
  445.9 8.1 %collective-permute-done.22 = bf16[4,256,256]{1,2,0:T(8,128)(2,1)S(1)} collective-permute-done((bf16[4,256,256]{1,2,0:T(8,128)(2,1)S(1)}, bf16[4,256,256]{1,2,0:T(8,128)(2,1)S(1)}, u32[]{:S(2)}, u32[]{:S(2)}) %collective-permute-start.22) | collective-permute-done | bytes 524320 | tf_op jit(solution)/shard_map/ppermute | solution.py:11
  457.1 10.3 %collective-permute-done.16 = bf16[4,256,256]{1,2,0:T(8,128)(2,1)S(1)} collective-permute-done((bf16[4,256,256]{1,2,0:T(8,128)(2,1)S(1)}, bf16[4,256,256]{1,2,0:T(8,128)(2,1)S(1)}, u32[]{:S(2)}, u32[]{:S(2)}) %collective-permute-start.16) | collective-permute-done | bytes 524320 | tf_op jit(solution)/shard_map/ppermute | solution.py:11
  468.7 9.3 %collective-permute-done.23 = bf16[4,256,256]{1,2,0:T(8,128)(2,1)S(1)} collective-permute-done((bf16[4,256,256]{1,2,0:T(8,128)(2,1)S(1)}, bf16[4,256,256]{1,2,0:T(8,128)(2,1)S(1)}, u32[]{:S(2)}, u32[]{:S(2)}) %collective-permute-start.23) | collective-permute-done | bytes 524320 | tf_op jit(solution)/shard_map/ppermute | solution.py:11
  482.1 10.9 %collective-permute-done.24 = bf16[4,256,256]{1,2,0:T(8,128)(2,1)S(1)} collective-permute-done((bf16[4,256,256]{1,2,0:T(8,128)(2,1)S(1)}, bf16[4,256,256]{1,2,0:T(8,128)(2,1)S(1)}, u32[]{:S(2)}, u32[]{:S(2)}) %collective-permute-start.24) | collective-permute-done | bytes 524320 | tf_op jit(solution)/shard_map/ppermute | solution.py:11
  494.9 10.8 %collective-permute-done.18 = bf16[4,256,256]{1,2,0:T(8,128)(2,1)S(1)} collective-permute-done((bf16[4,256,256]{1,2,0:T(8,128)(2,1)S(1)}, bf16[4,256,256]{1,2,0:T(8,128)(2,1)S(1)}, u32[]{:S(2)}, u32[]{:S(2)}) %collective-permute-start.18) | collective-permute-done | bytes 524320 | tf_op jit(solution)/shard_map/ppermute | solution.py:11
  506.3 9.0 %collective-permute-done.25 = bf16[4,256,256]{1,2,0:T(8,128)(2,1)S(1)} collective-permute-done((bf16[4,256,256]{1,2,0:T(8,128)(2,1)S(1)}, bf16[4,256,256]{1,2,0:T(8,128)(2,1)S(1)}, u32[]{:S(2)}, u32[]{:S(2)}) %collective-permute-start.25) | collective-permute-done | bytes 524320 | tf_op jit(solution)/shard_map/ppermute | solution.py:11
  518.9 11.4 %collective-permute-done.26 = bf16[4,256,256]{1,2,0:T(8,128)(2,1)S(1)} collective-permute-done((bf16[4,256,256]{1,2,0:T(8,128)(2,1)S(1)}, bf16[4,256,256]{1,2,0:T(8,128)(2,1)S(1)}, u32[]{:S(2)}, u32[]{:S(2)}) %collective-permute-start.26) | collective-permute-done | bytes 524320 | tf_op jit(solution)/shard_map/ppermute | solution.py:11
  533.3 9.1 %collective-permute-done.20 = bf16[4,256,256]{1,2,0:T(8,128)(2,1)S(1)} collective-permute-done((bf16[4,256,256]{1,2,0:T(8,128)(2,1)S(1)}, bf16[4,256,256]{1,2,0:T(8,128)(2,1)S(1)}, u32[]{:S(2)}, u32[]{:S(2)}) %collective-permute-start.20) | collective-permute-done | bytes 524320 | tf_op jit(solution)/shard_map/ppermute | solution.py:11
  543.5 7.8 %collective-permute-done.27 = bf16[4,256,256]{1,2,0:T(8,128)(2,1)} collective-permute-done((bf16[4,256,256]{1,2,0:T(8,128)(2,1)}, bf16[4,256,256]{1,2,0:T(8,128)(2,1)}, u32[]{:S(2)}, u32[]{:S(2)}) %collective-permute-start.27) | collective-permute-done | bytes 524320 | tf_op jit(solution)/shard_map/ppermute | solution.py:11
  (128 shorter events, 132.2 us)
Async XLA Ops:
  6.5 208.9 %all-gather.4.cloned.1.call-start = ((), (), s32[]{:S(2)}) async-start(), calls=%async_computation.1 | async-start | bytes 8454144 | tf_op jit(solution)/shard_map/all_gather | solution.py:92
  16.9 15.0 %collective-permute-start.1 = (bf16[4,256,256]{1,2,0:T(8,128)(2,1)S(1)}, bf16[4,256,256]{1,2,0:T(8,128)(2,1)}, u32[]{:S(2)}, u32[]{:S(2)}) collective-permute-start(bf16[4,256,256]{1,2,0:T(8,128)(2,1)S(1)} %broadcast_select_fusion.19), channel_id=1, source_target_pairs={{0,2},{1,3},{2,0},{3,1},{4,6},{5,7},{6,4},{7,5},{8,10},{9,11},{10,... | collective-permute-start | bytes 1572872 | tf_op jit(solution)/shard_map/ppermute | solution.py:11
  22.3 20.8 %collective-permute-start.8 = (bf16[4,256,256]{1,2,0:T(8,128)(2,1)S(1)}, bf16[4,256,256]{1,2,0:T(8,128)(2,1)}, u32[]{:S(2)}, u32[]{:S(2)}) collective-permute-start(bf16[4,256,256]{1,2,0:T(8,128)(2,1)S(1)} %broadcast_select_fusion.5), channel_id=1, source_target_pairs={{0,2},{1,3},{2,0},{3,1},{4,6},{5,7},{6,4},{7,5},{8,10},{9,11},{10,... | collective-permute-start | bytes 1572872 | tf_op jit(solution)/shard_map/ppermute | solution.py:11
  33.8 23.0 %collective-permute-start.2 = (bf16[4,256,256]{1,2,0:T(8,128)(2,1)}, bf16[4,256,256]{1,2,0:T(8,128)(2,1)S(1)}, u32[]{:S(2)}, u32[]{:S(2)}) collective-permute-start(bf16[4,256,256]{1,2,0:T(8,128)(2,1)} %broadcast_select_fusion.21), channel_id=1, source_target_pairs={{0,4},{1,5},{2,6},{3,7},{4,0},{5,1},{6,2},{7,3},{8,12},{9,13},{10,... | collective-permute-start | bytes 1572872 | tf_op jit(solution)/shard_map/ppermute | solution.py:11
  44.2 23.0 %collective-permute-start.9 = (bf16[4,256,256]{1,2,0:T(8,128)(2,1)S(1)}, bf16[4,256,256]{1,2,0:T(8,128)(2,1)}, u32[]{:S(2)}, u32[]{:S(2)}) collective-permute-start(bf16[4,256,256]{1,2,0:T(8,128)(2,1)S(1)} %broadcast_select_fusion.7), channel_id=1, source_target_pairs={{0,4},{1,5},{2,6},{3,7},{4,0},{5,1},{6,2},{7,3},{8,12},{9,13},{10,... | collective-permute-start | bytes 1572872 | tf_op jit(solution)/shard_map/ppermute | solution.py:11
  58.7 14.3 %collective-permute-start.3 = (bf16[4,256,256]{1,2,0:T(8,128)(2,1)}, bf16[4,256,256]{1,2,0:T(8,128)(2,1)}, u32[]{:S(2)}, u32[]{:S(2)}) collective-permute-start(bf16[4,256,256]{1,2,0:T(8,128)(2,1)} %broadcast_select_fusion.23), channel_id=1, source_target_pairs={{0,8},{1,9},{2,10},{3,11},{4,12},{5,13},{6,14},{7,15},{8,0},{9,1},... | collective-permute-start | bytes 1572872 | tf_op jit(solution)/shard_map/ppermute | solution.py:11
  67.3 16.9 %collective-permute-start.10 = (bf16[4,256,256]{1,2,0:T(8,128)(2,1)S(1)}, bf16[4,256,256]{1,2,0:T(8,128)(2,1)}, u32[]{:S(2)}, u32[]{:S(2)}) collective-permute-start(bf16[4,256,256]{1,2,0:T(8,128)(2,1)S(1)} %broadcast_select_fusion.9), channel_id=1, source_target_pairs={{0,8},{1,9},{2,10},{3,11},{4,12},{5,13},{6,14},{7,15},{8,0},{9,1},... | collective-permute-start | bytes 1572872 | tf_op jit(solution)/shard_map/ppermute | solution.py:11
  74.1 23.6 %collective-permute-start.4 = (bf16[4,256,256]{1,2,0:T(8,128)(2,1)S(1)}, bf16[4,256,256]{1,2,0:T(8,128)(2,1)}, u32[]{:S(2)}, u32[]{:S(2)}) collective-permute-start(bf16[4,256,256]{1,2,0:T(8,128)(2,1)S(1)} %broadcast_select_fusion.25), channel_id=1, source_target_pairs={{0,16},{1,17},{2,18},{3,19},{4,20},{5,21},{6,22},{7,23},{8,24},{9,... | collective-permute-start | bytes 1572872 | tf_op jit(solution)/shard_map/ppermute | solution.py:11
  85.4 21.7 %collective-permute-start.11 = (bf16[4,256,256]{1,2,0:T(8,128)(2,1)S(1)}, bf16[4,256,256]{1,2,0:T(8,128)(2,1)S(1)}, u32[]{:S(2)}, u32[]{:S(2)}) collective-permute-start(bf16[4,256,256]{1,2,0:T(8,128)(2,1)S(1)} %broadcast_select_fusion.11), channel_id=1, source_target_pairs={{0,16},{1,17},{2,18},{3,19},{4,20},{5,21},{6,22},{7,23},{8,24},{9,... | collective-permute-start | bytes 1572872 | tf_op jit(solution)/shard_map/ppermute | solution.py:11
  107.1 15.0 %collective-permute-start.12 = (bf16[4,256,256]{1,2,0:T(8,128)(2,1)S(1)}, bf16[4,256,256]{1,2,0:T(8,128)(2,1)}, u32[]{:S(2)}, u32[]{:S(2)}) collective-permute-start(bf16[4,256,256]{1,2,0:T(8,128)(2,1)S(1)} %broadcast_select_fusion.13), channel_id=1, source_target_pairs={{0,32},{1,33},{2,34},{3,35},{4,36},{5,37},{6,38},{7,39},{8,40},{9,... | collective-permute-start | bytes 1572872 | tf_op jit(solution)/shard_map/ppermute | solution.py:11
  110.6 26.3 %collective-permute-start.6 = (bf16[4,256,256]{1,2,0:T(8,128)(2,1)S(1)}, bf16[4,256,256]{1,2,0:T(8,128)(2,1)}, u32[]{:S(2)}, u32[]{:S(2)}) collective-permute-start(bf16[4,256,256]{1,2,0:T(8,128)(2,1)S(1)} %broadcast_select_fusion.29), channel_id=1, source_target_pairs={{0,64},{1,65},{2,66},{3,67},{4,68},{5,69},{6,70},{7,71},{8,72},{9,... | collective-permute-start | bytes 1572872 | tf_op jit(solution)/shard_map/ppermute | solution.py:11
  124.0 22.5 %collective-permute-start.13 = (bf16[4,256,256]{1,2,0:T(8,128)(2,1)}, bf16[4,256,256]{1,2,0:T(8,128)(2,1)}, u32[]{:S(2)}, u32[]{:S(2)}) collective-permute-start(bf16[4,256,256]{1,2,0:T(8,128)(2,1)} %broadcast_select_fusion.15), channel_id=1, source_target_pairs={{0,64},{1,65},{2,66},{3,67},{4,68},{5,69},{6,70},{7,71},{8,72},{9,... | collective-permute-start | bytes 1572872 | tf_op jit(solution)/shard_map/ppermute | solution.py:11
  151.1 173.0 %reduce-scatter.2.cloned.1.call-start = ((), (), s32[]{:S(2)}) async-start(), calls=%async_computation.2 | async-start | bytes 1179648 | tf_op jit(solution)/shard_map/reduce_scatter | solution.py:99
  294.5 110.5 %all-gather.6.cloned.1.call-start = ((), (), s32[]{:S(2)}) async-start(), calls=%async_computation.3 | async-start | bytes 8454144 | tf_op jit(solution)/shard_map/all_gather | solution.py:102
  427.9 14.8 %collective-permute-start.15 = (bf16[4,256,256]{1,2,0:T(8,128)(2,1)S(1)}, bf16[4,256,256]{1,2,0:T(8,128)(2,1)S(1)}, u32[]{:S(2)}, u32[]{:S(2)}) collective-permute-start(bf16[4,256,256]{1,2,0:T(8,128)(2,1)S(1)} %broadcast_select_fusion.18), channel_id=1, source_target_pairs={{0,2},{1,3},{2,0},{3,1},{4,6},{5,7},{6,4},{7,5},{8,10},{9,11},{10,... | collective-permute-start | bytes 1572872 | tf_op jit(solution)/shard_map/ppermute | solution.py:11
  429.6 24.4 %collective-permute-start.22 = (bf16[4,256,256]{1,2,0:T(8,128)(2,1)S(1)}, bf16[4,256,256]{1,2,0:T(8,128)(2,1)S(1)}, u32[]{:S(2)}, u32[]{:S(2)}) collective-permute-start(bf16[4,256,256]{1,2,0:T(8,128)(2,1)S(1)} %broadcast_select_fusion.4), channel_id=1, source_target_pairs={{0,2},{1,3},{2,0},{3,1},{4,6},{5,7},{6,4},{7,5},{8,10},{9,11},{10,... | collective-permute-start | bytes 1572872 | tf_op jit(solution)/shard_map/ppermute | solution.py:11
  442.8 24.6 %collective-permute-start.16 = (bf16[4,256,256]{1,2,0:T(8,128)(2,1)S(1)}, bf16[4,256,256]{1,2,0:T(8,128)(2,1)S(1)}, u32[]{:S(2)}, u32[]{:S(2)}) collective-permute-start(bf16[4,256,256]{1,2,0:T(8,128)(2,1)S(1)} %broadcast_select_fusion.20), channel_id=1, source_target_pairs={{0,4},{1,5},{2,6},{3,7},{4,0},{5,1},{6,2},{7,3},{8,12},{9,13},{10,... | collective-permute-start | bytes 1572872 | tf_op jit(solution)/shard_map/ppermute | solution.py:11
  454.0 23.9 %collective-permute-start.23 = (bf16[4,256,256]{1,2,0:T(8,128)(2,1)S(1)}, bf16[4,256,256]{1,2,0:T(8,128)(2,1)S(1)}, u32[]{:S(2)}, u32[]{:S(2)}) collective-permute-start(bf16[4,256,256]{1,2,0:T(8,128)(2,1)S(1)} %broadcast_select_fusion.6), channel_id=1, source_target_pairs={{0,4},{1,5},{2,6},{3,7},{4,0},{5,1},{6,2},{7,3},{8,12},{9,13},{10,... | collective-permute-start | bytes 1572872 | tf_op jit(solution)/shard_map/ppermute | solution.py:11
  478.0 14.9 %collective-permute-start.24 = (bf16[4,256,256]{1,2,0:T(8,128)(2,1)S(1)}, bf16[4,256,256]{1,2,0:T(8,128)(2,1)S(1)}, u32[]{:S(2)}, u32[]{:S(2)}) collective-permute-start(bf16[4,256,256]{1,2,0:T(8,128)(2,1)S(1)} %broadcast_select_fusion.8), channel_id=1, source_target_pairs={{0,8},{1,9},{2,10},{3,11},{4,12},{5,13},{6,14},{7,15},{8,0},{9,1},... | collective-permute-start | bytes 1572872 | tf_op jit(solution)/shard_map/ppermute | solution.py:11
  480.2 25.5 %collective-permute-start.18 = (bf16[4,256,256]{1,2,0:T(8,128)(2,1)S(1)}, bf16[4,256,256]{1,2,0:T(8,128)(2,1)S(1)}, u32[]{:S(2)}, u32[]{:S(2)}) collective-permute-start(bf16[4,256,256]{1,2,0:T(8,128)(2,1)S(1)} %broadcast_select_fusion.24), channel_id=1, source_target_pairs={{0,16},{1,17},{2,18},{3,19},{4,20},{5,21},{6,22},{7,23},{8,24},{9,... | collective-permute-start | bytes 1572872 | tf_op jit(solution)/shard_map/ppermute | solution.py:11
  493.0 22.3 %collective-permute-start.25 = (bf16[4,256,256]{1,2,0:T(8,128)(2,1)S(1)}, bf16[4,256,256]{1,2,0:T(8,128)(2,1)S(1)}, u32[]{:S(2)}, u32[]{:S(2)}) collective-permute-start(bf16[4,256,256]{1,2,0:T(8,128)(2,1)S(1)} %broadcast_select_fusion.10), channel_id=1, source_target_pairs={{0,16},{1,17},{2,18},{3,19},{4,20},{5,21},{6,22},{7,23},{8,24},{9,... | collective-permute-start | bytes 1572872 | tf_op jit(solution)/shard_map/ppermute | solution.py:11
  515.4 14.9 %collective-permute-start.26 = (bf16[4,256,256]{1,2,0:T(8,128)(2,1)S(1)}, bf16[4,256,256]{1,2,0:T(8,128)(2,1)S(1)}, u32[]{:S(2)}, u32[]{:S(2)}) collective-permute-start(bf16[4,256,256]{1,2,0:T(8,128)(2,1)S(1)} %broadcast_select_fusion.12), channel_id=1, source_target_pairs={{0,32},{1,33},{2,34},{3,35},{4,36},{5,37},{6,38},{7,39},{8,40},{9,... | collective-permute-start | bytes 1572872 | tf_op jit(solution)/shard_map/ppermute | solution.py:11
  516.7 25.8 %collective-permute-start.20 = (bf16[4,256,256]{1,2,0:T(8,128)(2,1)S(1)}, bf16[4,256,256]{1,2,0:T(8,128)(2,1)S(1)}, u32[]{:S(2)}, u32[]{:S(2)}) collective-permute-start(bf16[4,256,256]{1,2,0:T(8,128)(2,1)S(1)} %broadcast_select_fusion.28), channel_id=1, source_target_pairs={{0,64},{1,65},{2,66},{3,67},{4,68},{5,69},{6,70},{7,71},{8,72},{9,... | collective-permute-start | bytes 1572872 | tf_op jit(solution)/shard_map/ppermute | solution.py:11
  531.2 20.1 %collective-permute-start.27 = (bf16[4,256,256]{1,2,0:T(8,128)(2,1)}, bf16[4,256,256]{1,2,0:T(8,128)(2,1)}, u32[]{:S(2)}, u32[]{:S(2)}) collective-permute-start(bf16[4,256,256]{1,2,0:T(8,128)(2,1)} %broadcast_select_fusion.14), channel_id=1, source_target_pairs={{0,64},{1,65},{2,66},{3,67},{4,68},{5,69},{6,70},{7,71},{8,72},{9,... | collective-permute-start | bytes 1572872 | tf_op jit(solution)/shard_map/ppermute | solution.py:11
  (14 other events, 268.7 us)
Sparse Core Ops, SparseCore 0:
  151.2 64.2 all-gather.3
  294.7 29.3 reduce-scatter.1
  326.9 78.0 all-gather.5
where the time goes:
time: 569 us; the launch traced here: 567 us
  waiting for transfers between devices  321 us (56%)
  local copies, waits for them, and re-layouts  104 us (18%)
  starting transfers between devices  51.4 us (9%)
  blocking collectives  27.7 us (5%)
  other arithmetic  27.3 us (5%)
  between operations  18.8 us (3%)
  matrix products  18 us (3%)
    ppermute x28, waiting for transfers between devices, from_partner(): lax.ppermute(value, axis, [(i, i ^ 1 << apart) for i in range(lax.axis_si...  183 us
    scatter x1, local copies, waits for them, and re-layouts, shards(): jnp.zeros((all_map.shape[0], cases), jnp.bfloat16).at[all_map].set(all_rhs)  74.2 us
    all_gather x1, waiting for transfers between devices, shards(): coarse_full = lax.all_gather(own_rows, ('row', 'col'), axis=0, tiled=True)  71.5 us
    ppermute x28, starting transfers between devices, from_partner(): lax.ppermute(value, axis, [(i, i ^ 1 << apart) for i in range(lax.axis_si...  51.1 us
    all_gather x1, waiting for transfers between devices, shards(): lax.all_gather(restricted, ('row', 'col'), axis=0, tiled=True)  36.6 us
    reduce_scatter x1, waiting for transfers between devices, shards(): lax.psum_scatter(partial_sum, 'col', scatter_dimension=0, tiled=True)  29.3 us
    all_gather x1, blocking collectives, shards(): lax.all_gather(coarse_map, ('row', 'col'), axis=0, tiled=True)  27.7 us
    select_n x28, other arithmetic, travel(): carried = jnp.where(chosen, other, carried)  18.9 us
  transfers between devices with their start and end apart: 31, of which 28 were waited for; matrix products, arithmetic and copies ran while one was open for 5% of the time, Pallas kernels for 0%

commit v1 on v0

--- a/solution.py
+++ b/solution.py
@@ -2,6 +2,7 @@
 import jax.numpy as jnp
 from jax import lax
 from jax.sharding import PartitionSpec as P
+from jax.lax import all_to_all, axis_size
 
 MODES = 32
 SHARE = 256
@@ -89,7 +90,15 @@
     ).astype(jnp.bfloat16)
     restricted = restricted.reshape(count * MODES, cases)
     all_rhs, all_map = (
-        lax.all_gather(restricted, ("row", "col"), axis=0, tiled=True),
+        jnp.concatenate(
+            all_to_all(
+                jnp.stack([restricted for _ in range(axis_size(("row", "col")))]),
+                axis_name=("row", "col"),
+                split_axis=0,
+                concat_axis=0,
+            ),
+            0,
+        ),
         lax.all_gather(coarse_map, ("row", "col"), axis=0, tiled=True),
     )
     coarse_rhs = jnp.zeros((all_map.shape[0], cases), jnp.bfloat16).at[all_map].set(all_rhs)

time: 569 us -> 635 us (1.12)
  blocking collectives: 27.7 us -> 121 us
  waiting for transfers between devices: 321 us -> 284 us
    all_gather x1, blocking collectives: 27.7 us -> 121 us  [shards(): lax.all_gather(coarse_map, ('row', 'col'), axis=0, tiled=True)]
    all_gather x1 -> x0, waiting for transfers between devices: 36.6 us -> none  [shards(): lax.all_gather(restricted, ('row', 'col'), axis=0, tiled=True)]
  transfers between devices with their start and end apart: 31 -> 31, of which waited for: 28 -> 27; matrix products, arithmetic and copies ran while one was open for 5% -> 4% of each run, Pallas kernels for 0% -> 0%
where the time goes in v1:
time: 635 us; the launch traced here: 634 us
  waiting for transfers between devices  284 us (45%)
  blocking collectives  121 us (19%)
  local copies, waits for them, and re-layouts  108 us (17%)
  starting transfers between devices  57.5 us (9%)
  other arithmetic  27.3 us (4%)
  between operations  18.6 us (3%)
  matrix products  17.3 us (3%)
    ppermute x28, waiting for transfers between devices, from_partner(): lax.ppermute(value, axis, [(i, i ^ 1 << apart) for i in range(lax.axis_si...  183 us
    all_gather x1, blocking collectives, shards(): lax.all_gather(coarse_map, ('row', 'col'), axis=0, tiled=True)  121 us
    scatter x1, local copies, waits for them, and re-layouts, shards(): jnp.zeros((all_map.shape[0], cases), jnp.bfloat16).at[all_map].set(all_rhs)  74.2 us
    all_gather x1, waiting for transfers between devices, shards(): coarse_full = lax.all_gather(own_rows, ('row', 'col'), axis=0, tiled=True)  71.4 us
    ppermute x28, starting transfers between devices, from_partner(): lax.ppermute(value, axis, [(i, i ^ 1 << apart) for i in range(lax.axis_si...  51.1 us
    reduce_scatter x1, waiting for transfers between devices, shards(): lax.psum_scatter(partial_sum, 'col', scatter_dimension=0, tiled=True)  29.6 us
    select_n x28, other arithmetic, travel(): carried = jnp.where(chosen, other, carried)  18.9 us
  transfers between devices with their start and end apart: 31, of which 27 were waited for; matrix products, arithmetic and copies ran while one was open for 4% of the time, Pallas kernels for 0%

profile of v1, /device:TPU:0, one launch (start us, length us, event | category | flops | bytes accessed | tf_op | source)
XLA Modules:
  0.0 633.9 jit_solution(2983704863314774877)
XLA Ops:
  22.2 9.4 %collective-permute-done.1 = bf16[4,256,256]{1,2,0:T(8,128)(2,1)} collective-permute-done((bf16[4,256,256]{1,2,0:T(8,128)(2,1)S(1)}, bf16[4,256,256]{1,2,0:T(8,128)(2,1)}, u32[]{:S(2)}, u32[]{:S(2)}) %collective-permute-start.1) | collective-permute-done | bytes 524320 | tf_op jit(solution)/shard_map/ppermute | solution.py:12
  47.3 9.2 %collective-permute-done.2 = bf16[4,256,256]{1,2,0:T(8,128)(2,1)S(1)} collective-permute-done((bf16[4,256,256]{1,2,0:T(8,128)(2,1)}, bf16[4,256,256]{1,2,0:T(8,128)(2,1)S(1)}, u32[]{:S(2)}, u32[]{:S(2)}) %collective-permute-start.2) | collective-permute-done | bytes 524320 | tf_op jit(solution)/shard_map/ppermute | solution.py:12
  59.9 7.1 %collective-permute-done.9 = bf16[4,256,256]{1,2,0:T(8,128)(2,1)} collective-permute-done((bf16[4,256,256]{1,2,0:T(8,128)(2,1)S(1)}, bf16[4,256,256]{1,2,0:T(8,128)(2,1)}, u32[]{:S(2)}, u32[]{:S(2)}) %collective-permute-start.9) | collective-permute-done | bytes 524320 | tf_op jit(solution)/shard_map/ppermute | solution.py:12
  76.9 7.0 %collective-permute-done.10 = bf16[4,256,256]{1,2,0:T(8,128)(2,1)} collective-permute-done((bf16[4,256,256]{1,2,0:T(8,128)(2,1)S(1)}, bf16[4,256,256]{1,2,0:T(8,128)(2,1)}, u32[]{:S(2)}, u32[]{:S(2)}) %collective-permute-start.10) | collective-permute-done | bytes 524320 | tf_op jit(solution)/shard_map/ppermute | solution.py:12
  88.1 9.2 %collective-permute-done.4 = bf16[4,256,256]{1,2,0:T(8,128)(2,1)} collective-permute-done((bf16[4,256,256]{1,2,0:T(8,128)(2,1)S(1)}, bf16[4,256,256]{1,2,0:T(8,128)(2,1)}, u32[]{:S(2)}, u32[]{:S(2)}) %collective-permute-start.4) | collective-permute-done | bytes 524320 | tf_op jit(solution)/shard_map/ppermute | solution.py:12
  100.5 6.2 collective-permute-done.11
  114.1 7.7 %collective-permute-done.12 = bf16[4,256,256]{1,2,0:T(8,128)(2,1)} collective-permute-done((bf16[4,256,256]{1,2,0:T(8,128)(2,1)S(1)}, bf16[4,256,256]{1,2,0:T(8,128)(2,1)}, u32[]{:S(2)}, u32[]{:S(2)}) %collective-permute-start.12) | collective-permute-done | bytes 524320 | tf_op jit(solution)/shard_map/ppermute | solution.py:12
  127.6 8.9 %collective-permute-done.6 = bf16[4,256,256]{1,2,0:T(8,128)(2,1)} collective-permute-done((bf16[4,256,256]{1,2,0:T(8,128)(2,1)S(1)}, bf16[4,256,256]{1,2,0:T(8,128)(2,1)}, u32[]{:S(2)}, u32[]{:S(2)}) %collective-permute-start.6) | collective-permute-done | bytes 524320 | tf_op jit(solution)/shard_map/ppermute | solution.py:12
  160.5 120.8 %all-gather = s32[128,1,128]{2,1,0:T(1,128)S(1)} all-gather(s32[1,1,128]{2,1,0:T(1,128)S(1)} %bitcast.42), channel_id=1, replica_groups=mesh['row'=16,'col'=8] {'row','col'}, dimensions={0}, use_global_device_ids=true | all-gather | bytes 66048 | tf_op jit(solution)/shard_map/all_gather | solution.py:102
  281.4 74.2 %scatter_custom_fusion = bf16[16384,256]{1,0:T(8,128)(2,1)} fusion(s32[16384]{0:T(1024)S(1)} %compare_select_fusion, bf16[16384,256]{1,0:T(8,128)(2,1)} %bitcast.14, bf16[]{:T(256)} %constant.108.clone.1), kind=kCustom, calls=%fused_computation.8 | custom fusion | bytes 8389120 | tf_op jit(solution)/shard_map/scatter | solution.py:104
  360.7 29.6 %reduce-scatter.2.cloned.1.call-done = f32[128,256]{0,1:T(8,128)} async-done(((f32[1024,256]{0,1:T(8,128)}), f32[128,256]{0,1:T(8,128)}) %reduce-scatter.2.cloned.1.call-update) | async-done | bytes 131088 | tf_op jit(solution)/shard_map/reduce_scatter | solution.py:108
  392.0 7.7 %fusion.8 = f32[4,256,1024]{2,1,0:T(8,128)} fusion(bf16[4,1024,1024]{2,1,0:T(8,128)(2,1)} %param.11, bf16[4,1024,256]{1,2,0:T(8,128)(2,1)S(1)} %copy.17, bf16[4,256,256]{1,2,0:T(8,128)(2,1)S(1)} %pad_select_fusion.2, bf16[4,256,256]{1,2,0:T(8,128)(2,1)S(1)} %copy-done.4, f32[4,1024]{1,0:T(4,128)S(1)} %add_divide_fusion), kind=kOutput, calls=%fused_computation.59 | convolution fusion | flops 2154823680 | bytes 15745024 | tf_op jit(solution)/shard_map/sij,sjr->sir/dot_general | solution.py:85
  399.8 71.4 %all-gather.3.cloned.1.call-done = bf16[16384,256]{0,1:T(8,128)(2,1)} async-done(((bf16[128,256]{0,1:T(8,128)(2,1)}), bf16[16384,256]{0,1:T(8,128)(2,1)}) %all-gather.3.cloned.1.call-update) | async-done | bytes 8388624 | tf_op jit(solution)/shard_map/all_gather | solution.py:111
  471.2 11.9 %copy.23 = bf16[16384,256]{1,0:T(8,128)(2,1)} copy(bf16[16384,256]{0,1:T(8,128)(2,1)} %all-gather.3.cloned.1.call-done) | data formatting | bytes 16777216 | tf_op jit(solution)/shard_map/all_gather | solution.py:111
  496.4 12.5 %collective-permute-done.15 = bf16[4,256,256]{1,2,0:T(8,128)(2,1)S(1)} collective-permute-done((bf16[4,256,256]{1,2,0:T(8,128)(2,1)S(1)}, bf16[4,256,256]{1,2,0:T(8,128)(2,1)S(1)}, u32[]{:S(2)}, u32[]{:S(2)}) %collective-permute-start.15) | collective-permute-done | bytes 524320 | tf_op jit(solution)/shard_map/ppermute | solution.py:12
  512.0 8.1 %collective-permute-done.22 = bf16[4,256,256]{1,2,0:T(8,128)(2,1)S(1)} collective-permute-done((bf16[4,256,256]{1,2,0:T(8,128)(2,1)S(1)}, bf16[4,256,256]{1,2,0:T(8,128)(2,1)S(1)}, u32[]{:S(2)}, u32[]{:S(2)}) %collective-permute-start.22) | collective-permute-done | bytes 524320 | tf_op jit(solution)/shard_map/ppermute | solution.py:12
  523.3 10.3 %collective-permute-done.16 = bf16[4,256,256]{1,2,0:T(8,128)(2,1)S(1)} collective-permute-done((bf16[4,256,256]{1,2,0:T(8,128)(2,1)S(1)}, bf16[4,256,256]{1,2,0:T(8,128)(2,1)S(1)}, u32[]{:S(2)}, u32[]{:S(2)}) %collective-permute-start.16) | collective-permute-done | bytes 524320 | tf_op jit(solution)/shard_map/ppermute | solution.py:12
  534.8 9.3 %collective-permute-done.23 = bf16[4,256,256]{1,2,0:T(8,128)(2,1)S(1)} collective-permute-done((bf16[4,256,256]{1,2,0:T(8,128)(2,1)S(1)}, bf16[4,256,256]{1,2,0:T(8,128)(2,1)S(1)}, u32[]{:S(2)}, u32[]{:S(2)}) %collective-permute-start.23) | collective-permute-done | bytes 524320 | tf_op jit(solution)/shard_map/ppermute | solution.py:12
  548.2 10.9 %collective-permute-done.24 = bf16[4,256,256]{1,2,0:T(8,128)(2,1)S(1)} collective-permute-done((bf16[4,256,256]{1,2,0:T(8,128)(2,1)S(1)}, bf16[4,256,256]{1,2,0:T(8,128)(2,1)S(1)}, u32[]{:S(2)}, u32[]{:S(2)}) %collective-permute-start.24) | collective-permute-done | bytes 524320 | tf_op jit(solution)/shard_map/ppermute | solution.py:12
  561.0 10.8 %collective-permute-done.18 = bf16[4,256,256]{1,2,0:T(8,128)(2,1)S(1)} collective-permute-done((bf16[4,256,256]{1,2,0:T(8,128)(2,1)S(1)}, bf16[4,256,256]{1,2,0:T(8,128)(2,1)S(1)}, u32[]{:S(2)}, u32[]{:S(2)}) %collective-permute-start.18) | collective-permute-done | bytes 524320 | tf_op jit(solution)/shard_map/ppermute | solution.py:12
  572.5 9.0 %collective-permute-done.25 = bf16[4,256,256]{1,2,0:T(8,128)(2,1)S(1)} collective-permute-done((bf16[4,256,256]{1,2,0:T(8,128)(2,1)S(1)}, bf16[4,256,256]{1,2,0:T(8,128)(2,1)S(1)}, u32[]{:S(2)}, u32[]{:S(2)}) %collective-permute-start.25) | collective-permute-done | bytes 524320 | tf_op jit(solution)/shard_map/ppermute | solution.py:12
  585.0 11.4 %collective-permute-done.26 = bf16[4,256,256]{1,2,0:T(8,128)(2,1)S(1)} collective-permute-done((bf16[4,256,256]{1,2,0:T(8,128)(2,1)S(1)}, bf16[4,256,256]{1,2,0:T(8,128)(2,1)S(1)}, u32[]{:S(2)}, u32[]{:S(2)}) %collective-permute-start.26) | collective-permute-done | bytes 524320 | tf_op jit(solution)/shard_map/ppermute | solution.py:12
  599.5 9.1 %collective-permute-done.20 = bf16[4,256,256]{1,2,0:T(8,128)(2,1)S(1)} collective-permute-done((bf16[4,256,256]{1,2,0:T(8,128)(2,1)S(1)}, bf16[4,256,256]{1,2,0:T(8,128)(2,1)S(1)}, u32[]{:S(2)}, u32[]{:S(2)}) %collective-permute-start.20) | collective-permute-done | bytes 524320 | tf_op jit(solution)/shard_map/ppermute | solution.py:12
  609.6 7.8 %collective-permute-done.27 = bf16[4,256,256]{1,2,0:T(8,128)(2,1)} collective-permute-done((bf16[4,256,256]{1,2,0:T(8,128)(2,1)}, bf16[4,256,256]{1,2,0:T(8,128)(2,1)}, u32[]{:S(2)}, u32[]{:S(2)}) %collective-permute-start.27) | collective-permute-done | bytes 524320 | tf_op jit(solution)/shard_map/ppermute | solution.py:12
  (128 shorter events, 135.6 us)
Async XLA Ops:
  16.6 15.0 %collective-permute-start.1 = (bf16[4,256,256]{1,2,0:T(8,128)(2,1)S(1)}, bf16[4,256,256]{1,2,0:T(8,128)(2,1)}, u32[]{:S(2)}, u32[]{:S(2)}) collective-permute-start(bf16[4,256,256]{1,2,0:T(8,128)(2,1)S(1)} %broadcast_select_fusion.19), channel_id=1, source_target_pairs={{0,2},{1,3},{2,0},{3,1},{4,6},{5,7},{6,4},{7,5},{8,10},{9,11},{10,... | collective-permute-start | bytes 1572872 | tf_op jit(solution)/shard_map/ppermute | solution.py:12
  21.8 21.1 %collective-permute-start.8 = (bf16[4,256,256]{1,2,0:T(8,128)(2,1)S(1)}, bf16[4,256,256]{1,2,0:T(8,128)(2,1)}, u32[]{:S(2)}, u32[]{:S(2)}) collective-permute-start(bf16[4,256,256]{1,2,0:T(8,128)(2,1)S(1)} %broadcast_select_fusion.5), channel_id=1, source_target_pairs={{0,2},{1,3},{2,0},{3,1},{4,6},{5,7},{6,4},{7,5},{8,10},{9,11},{10,... | collective-permute-start | bytes 1572872 | tf_op jit(solution)/shard_map/ppermute | solution.py:12
  33.5 23.0 %collective-permute-start.2 = (bf16[4,256,256]{1,2,0:T(8,128)(2,1)}, bf16[4,256,256]{1,2,0:T(8,128)(2,1)S(1)}, u32[]{:S(2)}, u32[]{:S(2)}) collective-permute-start(bf16[4,256,256]{1,2,0:T(8,128)(2,1)} %broadcast_select_fusion.21), channel_id=1, source_target_pairs={{0,4},{1,5},{2,6},{3,7},{4,0},{5,1},{6,2},{7,3},{8,12},{9,13},{10,... | collective-permute-start | bytes 1572872 | tf_op jit(solution)/shard_map/ppermute | solution.py:12
  43.9 23.0 %collective-permute-start.9 = (bf16[4,256,256]{1,2,0:T(8,128)(2,1)S(1)}, bf16[4,256,256]{1,2,0:T(8,128)(2,1)}, u32[]{:S(2)}, u32[]{:S(2)}) collective-permute-start(bf16[4,256,256]{1,2,0:T(8,128)(2,1)S(1)} %broadcast_select_fusion.7), channel_id=1, source_target_pairs={{0,4},{1,5},{2,6},{3,7},{4,0},{5,1},{6,2},{7,3},{8,12},{9,13},{10,... | collective-permute-start | bytes 1572872 | tf_op jit(solution)/shard_map/ppermute | solution.py:12
  58.4 14.3 %collective-permute-start.3 = (bf16[4,256,256]{1,2,0:T(8,128)(2,1)}, bf16[4,256,256]{1,2,0:T(8,128)(2,1)}, u32[]{:S(2)}, u32[]{:S(2)}) collective-permute-start(bf16[4,256,256]{1,2,0:T(8,128)(2,1)} %broadcast_select_fusion.23), channel_id=1, source_target_pairs={{0,8},{1,9},{2,10},{3,11},{4,12},{5,13},{6,14},{7,15},{8,0},{9,1},... | collective-permute-start | bytes 1572872 | tf_op jit(solution)/shard_map/ppermute | solution.py:12
  67.0 16.9 %collective-permute-start.10 = (bf16[4,256,256]{1,2,0:T(8,128)(2,1)S(1)}, bf16[4,256,256]{1,2,0:T(8,128)(2,1)}, u32[]{:S(2)}, u32[]{:S(2)}) collective-permute-start(bf16[4,256,256]{1,2,0:T(8,128)(2,1)S(1)} %broadcast_select_fusion.9), channel_id=1, source_target_pairs={{0,8},{1,9},{2,10},{3,11},{4,12},{5,13},{6,14},{7,15},{8,0},{9,1},... | collective-permute-start | bytes 1572872 | tf_op jit(solution)/shard_map/ppermute | solution.py:12
  73.8 23.6 %collective-permute-start.4 = (bf16[4,256,256]{1,2,0:T(8,128)(2,1)S(1)}, bf16[4,256,256]{1,2,0:T(8,128)(2,1)}, u32[]{:S(2)}, u32[]{:S(2)}) collective-permute-start(bf16[4,256,256]{1,2,0:T(8,128)(2,1)S(1)} %broadcast_select_fusion.25), channel_id=1, source_target_pairs={{0,16},{1,17},{2,18},{3,19},{4,20},{5,21},{6,22},{7,23},{8,24},{9,... | collective-permute-start | bytes 1572872 | tf_op jit(solution)/shard_map/ppermute | solution.py:12
  85.0 21.7 %collective-permute-start.11 = (bf16[4,256,256]{1,2,0:T(8,128)(2,1)S(1)}, bf16[4,256,256]{1,2,0:T(8,128)(2,1)S(1)}, u32[]{:S(2)}, u32[]{:S(2)}) collective-permute-start(bf16[4,256,256]{1,2,0:T(8,128)(2,1)S(1)} %broadcast_select_fusion.11), channel_id=1, source_target_pairs={{0,16},{1,17},{2,18},{3,19},{4,20},{5,21},{6,22},{7,23},{8,24},{9,... | collective-permute-start | bytes 1572872 | tf_op jit(solution)/shard_map/ppermute | solution.py:12
  106.8 15.0 %collective-permute-start.12 = (bf16[4,256,256]{1,2,0:T(8,128)(2,1)S(1)}, bf16[4,256,256]{1,2,0:T(8,128)(2,1)}, u32[]{:S(2)}, u32[]{:S(2)}) collective-permute-start(bf16[4,256,256]{1,2,0:T(8,128)(2,1)S(1)} %broadcast_select_fusion.13), channel_id=1, source_target_pairs={{0,32},{1,33},{2,34},{3,35},{4,36},{5,37},{6,38},{7,39},{8,40},{9,... | collective-permute-start | bytes 1572872 | tf_op jit(solution)/shard_map/ppermute | solution.py:12
  110.2 26.3 %collective-permute-start.6 = (bf16[4,256,256]{1,2,0:T(8,128)(2,1)S(1)}, bf16[4,256,256]{1,2,0:T(8,128)(2,1)}, u32[]{:S(2)}, u32[]{:S(2)}) collective-permute-start(bf16[4,256,256]{1,2,0:T(8,128)(2,1)S(1)} %broadcast_select_fusion.29), channel_id=1, source_target_pairs={{0,64},{1,65},{2,66},{3,67},{4,68},{5,69},{6,70},{7,71},{8,72},{9,... | collective-permute-start | bytes 1572872 | tf_op jit(solution)/shard_map/ppermute | solution.py:12
  123.7 22.5 %collective-permute-start.13 = (bf16[4,256,256]{1,2,0:T(8,128)(2,1)}, bf16[4,256,256]{1,2,0:T(8,128)(2,1)}, u32[]{:S(2)}, u32[]{:S(2)}) collective-permute-start(bf16[4,256,256]{1,2,0:T(8,128)(2,1)} %broadcast_select_fusion.15), channel_id=1, source_target_pairs={{0,64},{1,65},{2,66},{3,67},{4,68},{5,69},{6,70},{7,71},{8,72},{9,... | collective-permute-start | bytes 1572872 | tf_op jit(solution)/shard_map/ppermute | solution.py:12
  154.4 127.0 %all-to-all-start = ((bf16[128,128,256]{2,1,0:T(8,128)(2,1)}), bf16[128,128,256]{2,1,0:T(8,128)(2,1)}, u32[]{:S(2)}, u32[]{:S(2)}) async-start(bf16[128,128,256]{2,1,0:T(8,128)(2,1)} %stack.3), calls=%async_computation | async-start | bytes 16777216 | tf_op jit(solution)/shard_map/all_to_all | solution.py:94
  160.5 229.9 %reduce-scatter.2.cloned.1.call-start = ((), (), s32[]{:S(2)}) async-start(), calls=%async_computation.2 | async-start | bytes 1179648 | tf_op jit(solution)/shard_map/reduce_scatter | solution.py:108
  360.4 110.7 %all-gather.3.cloned.1.call-start = ((), (), s32[]{:S(2)}) async-start(), calls=%async_computation.3 | async-start | bytes 8454144 | tf_op jit(solution)/shard_map/all_gather | solution.py:111
  494.0 14.8 %collective-permute-start.15 = (bf16[4,256,256]{1,2,0:T(8,128)(2,1)S(1)}, bf16[4,256,256]{1,2,0:T(8,128)(2,1)S(1)}, u32[]{:S(2)}, u32[]{:S(2)}) collective-permute-start(bf16[4,256,256]{1,2,0:T(8,128)(2,1)S(1)} %broadcast_select_fusion.18), channel_id=1, source_target_pairs={{0,2},{1,3},{2,0},{3,1},{4,6},{5,7},{6,4},{7,5},{8,10},{9,11},{10,... | collective-permute-start | bytes 1572872 | tf_op jit(solution)/shard_map/ppermute | solution.py:12
  495.7 24.4 %collective-permute-start.22 = (bf16[4,256,256]{1,2,0:T(8,128)(2,1)S(1)}, bf16[4,256,256]{1,2,0:T(8,128)(2,1)S(1)}, u32[]{:S(2)}, u32[]{:S(2)}) collective-permute-start(bf16[4,256,256]{1,2,0:T(8,128)(2,1)S(1)} %broadcast_select_fusion.4), channel_id=1, source_target_pairs={{0,2},{1,3},{2,0},{3,1},{4,6},{5,7},{6,4},{7,5},{8,10},{9,11},{10,... | collective-permute-start | bytes 1572872 | tf_op jit(solution)/shard_map/ppermute | solution.py:12
  508.9 24.6 %collective-permute-start.16 = (bf16[4,256,256]{1,2,0:T(8,128)(2,1)S(1)}, bf16[4,256,256]{1,2,0:T(8,128)(2,1)S(1)}, u32[]{:S(2)}, u32[]{:S(2)}) collective-permute-start(bf16[4,256,256]{1,2,0:T(8,128)(2,1)S(1)} %broadcast_select_fusion.20), channel_id=1, source_target_pairs={{0,4},{1,5},{2,6},{3,7},{4,0},{5,1},{6,2},{7,3},{8,12},{9,13},{10,... | collective-permute-start | bytes 1572872 | tf_op jit(solution)/shard_map/ppermute | solution.py:12
  520.2 23.9 %collective-permute-start.23 = (bf16[4,256,256]{1,2,0:T(8,128)(2,1)S(1)}, bf16[4,256,256]{1,2,0:T(8,128)(2,1)S(1)}, u32[]{:S(2)}, u32[]{:S(2)}) collective-permute-start(bf16[4,256,256]{1,2,0:T(8,128)(2,1)S(1)} %broadcast_select_fusion.6), channel_id=1, source_target_pairs={{0,4},{1,5},{2,6},{3,7},{4,0},{5,1},{6,2},{7,3},{8,12},{9,13},{10,... | collective-permute-start | bytes 1572872 | tf_op jit(solution)/shard_map/ppermute | solution.py:12
  544.2 14.9 %collective-permute-start.24 = (bf16[4,256,256]{1,2,0:T(8,128)(2,1)S(1)}, bf16[4,256,256]{1,2,0:T(8,128)(2,1)S(1)}, u32[]{:S(2)}, u32[]{:S(2)}) collective-permute-start(bf16[4,256,256]{1,2,0:T(8,128)(2,1)S(1)} %broadcast_select_fusion.8), channel_id=1, source_target_pairs={{0,8},{1,9},{2,10},{3,11},{4,12},{5,13},{6,14},{7,15},{8,0},{9,1},... | collective-permute-start | bytes 1572872 | tf_op jit(solution)/shard_map/ppermute | solution.py:12
  546.3 25.5 %collective-permute-start.18 = (bf16[4,256,256]{1,2,0:T(8,128)(2,1)S(1)}, bf16[4,256,256]{1,2,0:T(8,128)(2,1)S(1)}, u32[]{:S(2)}, u32[]{:S(2)}) collective-permute-start(bf16[4,256,256]{1,2,0:T(8,128)(2,1)S(1)} %broadcast_select_fusion.24), channel_id=1, source_target_pairs={{0,16},{1,17},{2,18},{3,19},{4,20},{5,21},{6,22},{7,23},{8,24},{9,... | collective-permute-start | bytes 1572872 | tf_op jit(solution)/shard_map/ppermute | solution.py:12
  559.2 22.3 %collective-permute-start.25 = (bf16[4,256,256]{1,2,0:T(8,128)(2,1)S(1)}, bf16[4,256,256]{1,2,0:T(8,128)(2,1)S(1)}, u32[]{:S(2)}, u32[]{:S(2)}) collective-permute-start(bf16[4,256,256]{1,2,0:T(8,128)(2,1)S(1)} %broadcast_select_fusion.10), channel_id=1, source_target_pairs={{0,16},{1,17},{2,18},{3,19},{4,20},{5,21},{6,22},{7,23},{8,24},{9,... | collective-permute-start | bytes 1572872 | tf_op jit(solution)/shard_map/ppermute | solution.py:12
  581.5 14.9 %collective-permute-start.26 = (bf16[4,256,256]{1,2,0:T(8,128)(2,1)S(1)}, bf16[4,256,256]{1,2,0:T(8,128)(2,1)S(1)}, u32[]{:S(2)}, u32[]{:S(2)}) collective-permute-start(bf16[4,256,256]{1,2,0:T(8,128)(2,1)S(1)} %broadcast_select_fusion.12), channel_id=1, source_target_pairs={{0,32},{1,33},{2,34},{3,35},{4,36},{5,37},{6,38},{7,39},{8,40},{9,... | collective-permute-start | bytes 1572872 | tf_op jit(solution)/shard_map/ppermute | solution.py:12
  582.8 25.8 %collective-permute-start.20 = (bf16[4,256,256]{1,2,0:T(8,128)(2,1)S(1)}, bf16[4,256,256]{1,2,0:T(8,128)(2,1)S(1)}, u32[]{:S(2)}, u32[]{:S(2)}) collective-permute-start(bf16[4,256,256]{1,2,0:T(8,128)(2,1)S(1)} %broadcast_select_fusion.28), channel_id=1, source_target_pairs={{0,64},{1,65},{2,66},{3,67},{4,68},{5,69},{6,70},{7,71},{8,72},{9,... | collective-permute-start | bytes 1572872 | tf_op jit(solution)/shard_map/ppermute | solution.py:12
  597.3 20.1 %collective-permute-start.27 = (bf16[4,256,256]{1,2,0:T(8,128)(2,1)}, bf16[4,256,256]{1,2,0:T(8,128)(2,1)}, u32[]{:S(2)}, u32[]{:S(2)}) collective-permute-start(bf16[4,256,256]{1,2,0:T(8,128)(2,1)} %broadcast_select_fusion.14), channel_id=1, source_target_pairs={{0,64},{1,65},{2,66},{3,67},{4,68},{5,69},{6,70},{7,71},{8,72},{9,... | collective-permute-start | bytes 1572872 | tf_op jit(solution)/shard_map/ppermute | solution.py:12
  (14 other events, 270.6 us)
Sparse Core Ops, SparseCore 0:
  360.6 29.7 reduce-scatter.1
  393.2 77.9 all-gather.2
